TPU v7x, 32 devices: a whole 2x2x4 slice. The times are simulated.
32 devices in a mesh: groups: 2 (over y), row: 4 (over z), col: 4 (over x, core).
Axes of the slice: x: 2, y: 2, z: 4, core: 2. Of those that a mesh axis runs over, the one named last changes fastest.
Arguments:
- slip: float32 [32, 16, 243], P(('groups', 'row', 'col')), parts along dimension 0, may hold values from -6 to 6
- inverse: float32 [32, 486, 243], P(('groups', 'row', 'col')), parts along dimension 0, may hold values from -0.6 to 0.6
- positions: float32 [32, 3, 81], P('groups'), parts along dimension 0
Outputs:
- updated: float32 [32, 16, 243], P(('groups', 'row', 'col')), parts along dimension 0
- residual: float32 [32, 16, 243], P(('groups', 'row', 'col')), parts along dimension 0
There are 2 independent parts, one for each index of `groups`. A program takes and returns all parts, laid end to end along the dimension named above; each array names one. Nothing has to cross between parts.
All inputs are finite; a program needn't handle non-finite values.
Results may differ from a plain program's by a relative error of at most 0.0041.
Values may be sent and summed in bfloat16 or wider, within the bound.
A program may use at most 64 MiB of HBM per device.

v0:
```python
import functools

import jax
import jax.numpy as jnp
from jax import lax
from jax.experimental import pallas as pl
from jax.experimental.pallas import tpu as pltpu
from jax.sharding import PartitionSpec as P

MESH = pl.DeviceIdType.MESH
LANES = 128
CHUNK = 16


def round_up(value, step):
    return -(-value // step) * step


def split(value):
    high = value.astype(jnp.bfloat16)
    low = (value - high.astype(jnp.float32)).astype(jnp.bfloat16)
    return high, low


def triple(rows, blobs, wide):
    lane = lax.broadcasted_iota(jnp.int32, rows.shape, rows.ndim - 1)
    axis = rows.ndim - 1
    once = pltpu.roll(rows, blobs, axis)
    twice = pltpu.roll(rows, 2 * blobs, axis)
    return jnp.where(lane < blobs, rows, jnp.where(lane < 2 * blobs, once, twice))


def kernel(
    row_count, col_count, blobs,
    slip_ref, inverse_ref, positions_ref,
    updated_ref, residual_ref,
    inverse_buf, inv_high, inv_low, tiles, own, source, other_slip, other_res, forces,
    inverse_sem, slip_sems, res_sems, send_sems, recv_sems,
):
    count = row_count * col_count
    row = lax.axis_index("row")
    col = lax.axis_index("col")
    me = row * col_count + col
    half = col % 2
    partner = col + 1 - 2 * half
    narrow = 3 * blobs
    wide = source.shape[-1]
    pad = own.shape[1]

    load = pltpu.make_async_copy(inverse_ref.at[0], inverse_buf, inverse_sem)
    load.start()

    barrier = pltpu.get_barrier_semaphore()

    def place(step):
        there = lax.rem(me + step, count)
        return there, {"row": there // col_count, "col": lax.rem(there, col_count)}

    def greet(step, carry):
        pl.semaphore_signal(barrier, inc=1, device_id=place(step)[1], device_id_type=MESH)
        return carry

    lax.fori_loop(1, count, greet, 0)

    def prepare(q, carry):
        rows = jnp.pad(positions_ref[q], ((0, 5), (0, wide - blobs)))
        spread = triple(rows, blobs, wide)
        lane = lax.broadcasted_iota(jnp.int32, (1, wide), 1)
        mixed = jnp.where(
            lane < blobs, spread[0:1], jnp.where(lane < 2 * blobs, spread[1:2], spread[2:3])
        )
        source[q, 0:3, :] = spread[0:3]
        source[q, 3:4, :] = mixed
        return carry

    lax.fori_loop(0, count, prepare, 0)
    own_rows = jnp.pad(positions_ref[me], ((0, 5), (0, LANES - blobs)))
    own_cols = own_rows.T
    lane = lax.broadcasted_iota(jnp.int32, (pad, wide), 1)
    parts = [jnp.broadcast_to(own_cols[:pad, a : a + 1], (pad, wide)) for a in range(3)]
    for a in range(3):
        own[a] = parts[a]
    own[3] = jnp.where(lane < blobs, parts[0], jnp.where(lane < 2 * blobs, parts[1], parts[2]))

    def build(q, carry):
        lane = lax.broadcasted_iota(jnp.int32, (CHUNK, wide), 1)
        masks = [(lane >= a * blobs) & (lane < (a + 1) * blobs) for a in range(3)]
        there = [jnp.broadcast_to(source[q, a : a + 1, :], (CHUNK, wide)) for a in range(4)]
        for at in range(0, pad, CHUNK):
            d0, d1, d2, db = [own[a, at : at + CHUNK, :] - there[a] for a in range(4)]
            dist_sq = d0 * d0 + d1 * d1 + d2 * d2
            r = lax.rsqrt(jnp.where(dist_sq > 0.0, dist_sq, 1.0))
            r2 = r * r
            t = 0.75 * r
            u = t * r2
            far = dist_sq >= 4.0
            isotropic = jnp.where(far, t + (2.0 / 3.0) * u, 1.0 - (9.0 / 32.0) * (dist_sq * r))
            anisotropic = jnp.where(far, u - (2.0 * u) * r2, (3.0 / 32.0) * r)
            scaled = anisotropic * db
            for a, da in enumerate((d0, d1, d2)):
                value = scaled * da + jnp.where(masks[a], isotropic, 0.0)
                tiles[q, a * pad + at : a * pad + at + CHUNK, :] = value.astype(jnp.bfloat16)
        return carry

    lax.fori_loop(0, count // 2, build, 0)

    pl.semaphore_wait(barrier, count - 1)

    def swap(source_ref, target_ref, sems):
        return pltpu.make_async_remote_copy(
            src_ref=source_ref,
            dst_ref=target_ref,
            send_sem=sems.at[0],
            recv_sem=sems.at[1],
            device_id={"col": partner},
            device_id_type=MESH,
        )

    slip_swap = swap(slip_ref.at[0], other_slip, slip_sems)
    slip_swap.start()

    load.wait()
    inv_high[...] = jnp.zeros_like(inv_high)
    inv_low[...] = jnp.zeros_like(inv_low)
    for h in range(2):
        high, low = split(inverse_buf[h * narrow : (h + 1) * narrow, :])
        inv_high[h, :narrow, :narrow] = high
        inv_low[h, :narrow, :narrow] = low

    def apply(values, h):
        high, low = split(values)
        big = inv_high[h, :narrow, :]
        small = inv_low[h, :narrow, :]
        rows = values.shape[0]
        both = jnp.dot(
            jnp.concatenate([high, low], axis=0), big, preferred_element_type=jnp.float32
        )
        cross = jnp.dot(high, small, preferred_element_type=jnp.float32)
        return both[:rows] + (both[rows:] + cross)

    force = apply(slip_ref[0], half)
    slip_swap.wait()
    force = force + apply(other_slip[...], 1 - half)
    forces[me] = force.astype(jnp.bfloat16)

    def send(step):
        there, device = place(step)
        return pltpu.make_async_remote_copy(
            src_ref=forces.at[me],
            dst_ref=forces.at[me],
            send_sem=send_sems.at[step],
            recv_sem=recv_sems.at[me],
            device_id=device,
            device_id_type=MESH,
        )

    def start_send(step, carry):
        send(step).start()
        return carry

    lax.fori_loop(1, count, start_send, 0)

    lax.fori_loop(count // 2, count, build, 0)

    def receive(q):
        pltpu.make_async_remote_copy(
            src_ref=forces.at[q],
            dst_ref=forces.at[q],
            send_sem=send_sems.at[0],
            recv_sem=recv_sems.at[q],
            device_id={"col": partner},
            device_id_type=MESH,
        ).wait_recv()

    def product(q):
        return lax.dot_general(
            forces[q], tiles[q], (((1,), (1,)), ((), ())), preferred_element_type=jnp.float32
        )

    def gather(turn, total):
        for c in range(col_count):
            step = turn * col_count + c
            q = lax.rem(me + step, count)

            @pl.when(step > 0)
            def _():
                receive(q)

            total = total + product(q)
        return total

    rows = slip_ref.shape[1]
    total = lax.fori_loop(0, row_count, gather, jnp.zeros((rows, 3 * pad), jnp.float32))
    total = jnp.pad(total, ((0, 0), (0, round_up(3 * pad, LANES) - 3 * pad)))
    full = total.shape[1]
    lane = lax.broadcasted_iota(jnp.int32, total.shape, 1)
    shift = pad - blobs
    velocity = jnp.where(
        lane < blobs,
        total,
        jnp.where(
            lane < 2 * blobs,
            pltpu.roll(total, full - shift, 1),
            pltpu.roll(total, full - 2 * shift, 1),
        ),
    )
    residual = slip_ref[0] - velocity[:, :narrow]
    residual_ref[0] = residual
    res_swap = swap(residual_ref.at[0], other_res, res_sems)
    res_swap.start()
    updated = force + apply(residual, half)

    def end_send(step, carry):
        send(step).wait_send()
        return carry

    lax.fori_loop(1, count, end_send, 0)
    res_swap.wait()
    updated = updated + apply(other_res[...], 1 - half)
    updated_ref[0] = updated[:, :narrow]


def local(slip, inverse, positions):
    row_count = lax.axis_size("row")
    col_count = lax.axis_size("col")
    count = row_count * col_count
    blobs = positions.shape[2]
    rows, narrow = slip.shape[1:]
    wide = round_up(narrow, LANES)
    pad = round_up(blobs, CHUNK)
    vmem = pl.BlockSpec(memory_space=pltpu.VMEM)
    f32, bf16 = jnp.float32, jnp.bfloat16
    updated, residual = pl.pallas_call(
        functools.partial(kernel, row_count, col_count, blobs),
        out_shape=(
            jax.ShapeDtypeStruct(slip.shape, f32),
            jax.ShapeDtypeStruct(slip.shape, f32),
        ),
        in_specs=[vmem, pl.BlockSpec(memory_space=pl.ANY), vmem],
        out_specs=(vmem, vmem),
        scratch_shapes=[
            pltpu.VMEM(inverse.shape[1:], f32),
            pltpu.VMEM((2, round_up(narrow, CHUNK), wide), bf16),
            pltpu.VMEM((2, round_up(narrow, CHUNK), wide), bf16),
            pltpu.VMEM((count, 3 * pad, wide), bf16),
            pltpu.VMEM((4, pad, wide), f32),
            pltpu.VMEM((count, 8, wide), f32),
            pltpu.VMEM((rows, narrow), f32),
            pltpu.VMEM((rows, narrow), f32),
            pltpu.VMEM((count, rows, wide), bf16),
            pltpu.SemaphoreType.DMA,
            pltpu.SemaphoreType.DMA((2,)),
            pltpu.SemaphoreType.DMA((2,)),
            pltpu.SemaphoreType.DMA((count,)),
            pltpu.SemaphoreType.DMA((count,)),
        ],
        compiler_params=pltpu.CompilerParams(
            collective_id=0, has_side_effects=True, vmem_limit_bytes=60 * 1024 * 1024
        ),
    )(slip, inverse, positions)
    return updated, residual


def solution(mesh):
    in_specs = (
        P(("groups", "row", "col"), None, None),
        P(("groups", "row", "col"), None, None),
        P("groups", None, None),
    )
    out_specs = (P(("groups", "row", "col"), None, None), P(("groups", "row", "col"), None, None))
    return jax.shard_map(local, mesh=mesh, in_specs=in_specs, out_specs=out_specs, check_vma=False)
```

profile of v0, /device:TPU:0, one launch (start us, length us, event | category | flops | bytes accessed | tf_op | source)
XLA Modules:
  0.0 20.6 jit_solution(8075703846109903516)
XLA Ops:
  0.6 1.4 %copy.6.positions_ref = f32[16,3,81]{2,1,0:T(4,128)} copy(f32[16,3,81]{2,0,1:T(8,128)} %param.5) | data formatting | bytes 31104 | tf_op args[2]
  2.0 1.8 %copy.5.inverse_ref = f32[1,486,243]{2,1,0:T(8,128)} copy(f32[1,486,243]{2,0,1:T(1,128)} %param.4) | data formatting | bytes 944784 | tf_op args[1]
  3.8 14.8 %shard_map.50 = (f32[1,16,243]{2,1,0:T(8,128)}, f32[1,16,243]{2,1,0:T(8,128)}) custom-call(f32[1,16,243]{2,1,0:T(8,128)} %slip_ref.1, f32[1,486,243]{2,1,0:T(8,128)} %copy.5.inverse_ref, f32[16,3,81]{2,1,0:T(4,128)} %copy.6.positions_ref), custom_call_target="tpu_custom_call" | custom-call | tf_op jit(solution)/shard_map/pallas_call | solution.py:233
  18.6 0.0 copy-start
  18.6 1.3 %copy.9 = f32[1,16,243]{2,1,0:T(8,128)} copy(f32[1,16,243]{2,1,0:T(8,128)} %get-tuple-element.4) | data formatting | bytes 31104
  20.0 0.0 copy-done
  20.0 0.6 %copy.10 = f32[1,16,243]{2,1,0:T(8,128)} copy(f32[1,16,243]{2,1,0:T(8,128)S(1)} %copy-done) | data formatting | bytes 31104
Async XLA Ops:
  18.6 1.3 %copy-start = (f32[1,16,243]{2,1,0:T(8,128)S(1)}, f32[1,16,243]{2,1,0:T(8,128)}, u32[]{:S(2)}) copy-start(f32[1,16,243]{2,1,0:T(8,128)} %get-tuple-element.5) | copy-start | bytes 46660
where the time goes:
time: 20.9 us; the launch traced here: 20.6 us
  Pallas kernels  14.8 us (71%)
  local copies, waits for them, and re-layouts  5.14 us (25%)
  between operations  0.65 us (3%)
    pallas_call x1, Pallas kernels, local(): pl.pallas_call(functools.partial(kernel, row_count, col_count, blobs), ou...  14.8 us
    unnamed x6, local copies, waits for them, and re-layouts  5.14 us

commit v1 on v0

v1 whole, which is shorter than its diff:
```python
import functools

import jax
import jax.numpy as jnp
from jax import lax
from jax.experimental import pallas as pl
from jax.experimental.pallas import tpu as pltpu
from jax.sharding import PartitionSpec as P

MESH = pl.DeviceIdType.MESH
LANES = 128
CHUNK = 16


def round_up(value, step):
    return -(-value // step) * step


def split(value):
    high = value.astype(jnp.bfloat16)
    low = (value - high.astype(jnp.float32)).astype(jnp.bfloat16)
    return high, low


def triple(rows, blobs):
    lane = lax.broadcasted_iota(jnp.int32, rows.shape, rows.ndim - 1)
    axis = rows.ndim - 1
    once = pltpu.roll(rows, blobs, axis)
    twice = pltpu.roll(rows, 2 * blobs, axis)
    return jnp.where(lane < blobs, rows, jnp.where(lane < 2 * blobs, once, twice))


def kernel(
    row_count, col_count, blobs,
    slip_hbm, inverse_hbm, positions_hbm,
    updated, residual,
    slip, inverse, positions,
    inv_high, inv_low, tiles, own_rows, own, source, other_slip, part, other_part, forces, held,
    load_sems, slip_sems, part_sems, send_sems, recv_sems,
):
    bodies = row_count * col_count // 2
    row = lax.axis_index("row")
    col = lax.axis_index("col")
    half = lax.rem(col, 2)
    partner = col + 1 - 2 * half
    body = (row * col_count + col) // 2
    narrow = 3 * blobs
    wide = source.shape[-1]
    pad = own.shape[2]

    barrier = pltpu.get_barrier_semaphore()

    def place(step):
        there = 2 * lax.rem(body + step, bodies) + half
        return {"row": there // col_count, "col": lax.rem(there, col_count)}

    def greet(step, carry):
        pl.semaphore_signal(barrier, inc=1, device_id=place(step), device_id_type=MESH)
        return carry

    pl.semaphore_signal(barrier, inc=1, device_id={"col": partner}, device_id_type=MESH)
    lax.fori_loop(1, bodies, greet, 0)

    loads = [
        pltpu.make_async_copy(positions_hbm, positions, load_sems.at[0]),
        pltpu.make_async_copy(slip_hbm.at[0], slip, load_sems.at[1]),
        pltpu.make_async_copy(inverse_hbm.at[:, 0, :], inverse, load_sems.at[2]),
    ]
    for load in loads:
        load.start()
    inv_high[...] = jnp.zeros_like(inv_high)
    inv_low[...] = jnp.zeros_like(inv_low)
    own_rows[...] = jnp.zeros_like(own_rows)
    loads[0].wait()

    lane = lax.broadcasted_iota(jnp.int32, source.shape[1:], 1)
    spread = []
    for a in range(3):
        rows = jnp.pad(positions[a], ((0, 0), (0, wide - blobs)))
        spread.append(triple(rows, blobs))
        source[a] = spread[a]
        for t in range(2):
            own_rows[3 * t + a : 3 * t + a + 1, :blobs] = positions[a, pl.ds(2 * body + t, 1), :]
    source[3] = jnp.where(
        lane < blobs, spread[0], jnp.where(lane < 2 * blobs, spread[1], spread[2])
    )
    own_cols = own_rows[...].T
    lane = lax.broadcasted_iota(jnp.int32, (pad, wide), 1)
    for t in range(2):
        cols = [
            jnp.broadcast_to(own_cols[:pad, 3 * t + a : 3 * t + a + 1], (pad, wide))
            for a in range(3)
        ]
        for a in range(3):
            own[t, a] = cols[a]
        own[t, 3] = jnp.where(lane < blobs, cols[0], jnp.where(lane < 2 * blobs, cols[1], cols[2]))

    def build(step, carry):
        j = step // 2
        t = lax.rem(step, 2)
        lane = lax.broadcasted_iota(jnp.int32, (CHUNK, wide), 1)
        masks = [(lane >= a * blobs) & (lane < (a + 1) * blobs) for a in range(3)]
        there = [
            jnp.broadcast_to(source[a, pl.ds(2 * j + half, 1), :], (CHUNK, wide)) for a in range(4)
        ]
        for at in range(0, pad, CHUNK):
            d0, d1, d2, db = [own[t, a, at : at + CHUNK, :] - there[a] for a in range(4)]
            dist_sq = d0 * d0 + d1 * d1 + d2 * d2
            r = lax.rsqrt(jnp.where(dist_sq > 0.0, dist_sq, 1.0))
            r2 = r * r
            k = 0.75 * r
            u = k * r2
            far = dist_sq >= 4.0
            isotropic = jnp.where(far, k + (2.0 / 3.0) * u, 1.0 - (9.0 / 32.0) * (dist_sq * r))
            anisotropic = jnp.where(far, u - (2.0 * u) * r2, (3.0 / 32.0) * r)
            scaled = anisotropic * db
            for a, da in enumerate((d0, d1, d2)):
                value = scaled * da + jnp.where(masks[a], isotropic, 0.0)
                tiles[j, t, a * pad + at : a * pad + at + CHUNK, :] = value.astype(jnp.bfloat16)
        return carry

    first = bodies
    lax.fori_loop(0, first, build, 0)
    loads[1].wait()
    pl.semaphore_wait(barrier, bodies)

    def swap(source_ref, target_ref, sems):
        return pltpu.make_async_remote_copy(
            src_ref=source_ref,
            dst_ref=target_ref,
            send_sem=sems.at[0],
            recv_sem=sems.at[1],
            device_id={"col": partner},
            device_id_type=MESH,
        )

    slip_swap = swap(slip, other_slip, slip_sems)
    slip_swap.start()

    loads[2].wait()
    for h in range(2):
        high, low = split(inverse[h * narrow : (h + 1) * narrow, :])
        inv_high[h, :narrow, :narrow] = high
        inv_low[h, :narrow, :narrow] = low

    def apply(values, h):
        high, low = split(jnp.pad(values, ((0, 0), (0, wide - narrow))))
        big = inv_high[h]
        small = inv_low[h]
        rows = values.shape[0]
        both = jnp.dot(
            jnp.concatenate([high, low], axis=0), big, preferred_element_type=jnp.float32
        )
        cross = jnp.dot(high, small, preferred_element_type=jnp.float32)
        return both[:rows] + (both[rows:] + cross)

    force = apply(slip[...], half)
    slip_swap.wait()
    force = force + apply(other_slip[...], 1 - half)
    forces[body] = force.astype(jnp.bfloat16)
    held[...] = force

    def send(step):
        return pltpu.make_async_remote_copy(
            src_ref=forces.at[body],
            dst_ref=forces.at[body],
            send_sem=send_sems.at[step],
            recv_sem=recv_sems.at[body],
            device_id=place(step),
            device_id_type=MESH,
        )

    def start_send(step, carry):
        send(step).start()
        return carry

    lax.fori_loop(1, bodies, start_send, 0)

    lax.fori_loop(first, 2 * bodies, build, 0)

    def product(j):
        return lax.dot_general(
            forces[j],
            tiles[j].reshape(6 * pad, wide),
            (((1,), (1,)), ((), ())),
            preferred_element_type=jnp.float32,
        )

    def gather(step, total):
        j = lax.rem(body + step, bodies)
        pltpu.make_async_remote_copy(
            src_ref=forces.at[j],
            dst_ref=forces.at[j],
            send_sem=send_sems.at[0],
            recv_sem=recv_sems.at[j],
            device_id={"col": partner},
            device_id_type=MESH,
        ).wait_recv()
        return total + product(j)

    total = product(body)
    if bodies <= 8:
        for step in range(1, bodies):
            total = gather(step, total)
    else:
        total = lax.fori_loop(1, bodies, gather, total)
    full = round_up(6 * pad, LANES)
    total = jnp.pad(total, ((0, 0), (0, full - 6 * pad)))
    lane = lax.broadcasted_iota(jnp.int32, total.shape, 1)

    def moved(by):
        return pltpu.roll(total, full - by, 1) if by else total

    for t in range(2):
        start = 3 * t * pad
        shift = pad - blobs
        value = jnp.where(
            lane < blobs,
            moved(start),
            jnp.where(lane < 2 * blobs, moved(start + shift), moved(start + 2 * shift)),
        )
        part[t] = value[:, :wide]
    part_swap = swap(part, other_part, part_sems)
    part_swap.start()

    def end_send(step, carry):
        send(step).wait_send()
        return carry

    lax.fori_loop(1, bodies, end_send, 0)
    part_swap.wait()
    mine = slip[...] - (part[half] + other_part[half])[:, :narrow]
    residual[0] = mine
    theirs = other_slip[...] - (part[1 - half] + other_part[1 - half])[:, :narrow]
    result = held[...] + (apply(mine, half) + apply(theirs, 1 - half))
    updated[0] = result[:, :narrow]


def finish(updated, residual, updated_out, residual_out, sems):
    copies = [
        pltpu.make_async_copy(updated, updated_out, sems.at[0]),
        pltpu.make_async_copy(residual, residual_out, sems.at[1]),
    ]
    for copy in copies:
        copy.start()
    for copy in copies:
        copy.wait()


def stay(value):
    return pltpu.with_memory_space_constraint(value, pltpu.HBM)


def local(slip, inverse, positions):
    row_count = lax.axis_size("row")
    col_count = lax.axis_size("col")
    count = row_count * col_count
    bodies = count // 2
    blobs = positions.shape[2]
    rows, narrow = slip.shape[1:]
    wide = round_up(narrow, LANES)
    pad = round_up(blobs, CHUNK)
    vmem = pl.BlockSpec(memory_space=pltpu.VMEM)
    f32, bf16 = jnp.float32, jnp.bfloat16
    dma = pltpu.SemaphoreType.DMA
    tile_bytes = bodies * 6 * pad * wide * 2
    updated, residual = pl.pallas_call(
        functools.partial(kernel, row_count, col_count, blobs),
        out_shape=(
            pltpu.VMEM(slip.shape, f32),
            pltpu.VMEM(slip.shape, f32),
        ),
        in_specs=[pl.BlockSpec(memory_space=pltpu.HBM)] * 3,
        out_specs=(vmem, vmem),
        scratch_shapes=[
            pltpu.VMEM((rows, narrow), f32),
            pltpu.VMEM(inverse.shape[1:], f32),
            pltpu.VMEM((3, count, blobs), f32),
            pltpu.VMEM((2, wide, wide), bf16),
            pltpu.VMEM((2, wide, wide), bf16),
            pltpu.VMEM((bodies, 2, 3 * pad, wide), bf16),
            pltpu.VMEM((8, LANES), f32),
            pltpu.VMEM((2, 4, pad, wide), f32),
            pltpu.VMEM((4, count, wide), f32),
            pltpu.VMEM((rows, narrow), f32),
            pltpu.VMEM((2, rows, wide), f32),
            pltpu.VMEM((2, rows, wide), f32),
            pltpu.VMEM((bodies, rows, wide), bf16),
            pltpu.VMEM((rows, wide), f32),
            dma((3,)),
            dma((2,)),
            dma((2,)),
            dma((bodies,)),
            dma((bodies,)),
        ],
        compiler_params=pltpu.CompilerParams(
            collective_id=0,
            has_side_effects=True,
            vmem_limit_bytes=2 * tile_bytes if 2 * tile_bytes < 2**24 else 60 * 2**20,
        ),
    )(*(stay(v) for v in (slip, jnp.swapaxes(inverse, 0, 1), jnp.swapaxes(positions, 0, 1))))
    return pl.pallas_call(
        finish,
        out_shape=(jax.ShapeDtypeStruct(slip.shape, f32),) * 2,
        in_specs=[vmem, vmem],
        out_specs=(pl.BlockSpec(memory_space=pltpu.HBM),) * 2,
        scratch_shapes=[dma((2,))],
        compiler_params=pltpu.CompilerParams(vmem_limit_bytes=2**20),
    )(updated, residual)


def solution(mesh):
    in_specs = (
        P(("groups", "row", "col"), None, None),
        P(("groups", "row", "col"), None, None),
        P("groups", None, None),
    )
    out_specs = (P(("groups", "row", "col"), None, None), P(("groups", "row", "col"), None, None))
    return jax.shard_map(local, mesh=mesh, in_specs=in_specs, out_specs=out_specs, check_vma=False)
```

time: 20.9 us -> 14.1 us (0.67)
  local copies, waits for them, and re-layouts: 5.14 us -> 0 us
  Pallas kernels: 14.8 us -> 13.3 us
    unnamed x6 -> x0, local copies, waits for them, and re-layouts: 5.14 us -> none
    pallas_call x1, Pallas kernels: 14.8 us -> 12.7 us  [local(): pl.pallas_call(functools.partial(kernel, row_count, col_count, blobs), ou...]
    pallas_call x0 -> x1, Pallas kernels: none -> 0.63 us  [local(): pl.pallas_call(finish, out_shape=(jax.ShapeDtypeStruct(slip.shape, f32),)...]
where the time goes in v1:
time: 14.1 us; the launch traced here: 13.9 us
  Pallas kernels  13.3 us (94%)
  between operations  0.64 us (5%)
    pallas_call x1, Pallas kernels, local(): pl.pallas_call(functools.partial(kernel, row_count, col_count, blobs), ou...  12.7 us
    pallas_call x1, Pallas kernels, local(): pl.pallas_call(finish, out_shape=(jax.ShapeDtypeStruct(slip.shape, f32),)...  0.63 us

profile of v1, /device:TPU:0, one launch (start us, length us, event | category | flops | bytes accessed | tf_op | source)
XLA Modules:
  0.0 13.9 jit_solution(16469787166944644439)
XLA Ops:
  0.6 12.7 %shard_map.50 = (f32[1,16,243]{2,1,0:T(8,128)S(1)}, f32[1,16,243]{2,1,0:T(8,128)S(1)}) custom-call(f32[1,16,243]{2,1,0:T(8,128)} %slip_hbm.1, f32[486,1,243]{2,1,0:T(1,128)} %bitcast.2, f32[3,16,81]{2,1,0:T(8,128)} %bitcast.3), custom_call_target="tpu_custom_call" | custom-call | tf_op jit(solution)/shard_map/pallas_call | solution.py:267
  13.3 0.6 %shard_map.51 = (f32[1,16,243]{2,1,0:T(8,128)}, f32[1,16,243]{2,1,0:T(8,128)}) custom-call(f32[1,16,243]{2,1,0:T(8,128)S(1)} %get-tuple-element.4.updated, f32[1,16,243]{2,1,0:T(8,128)S(1)} %get-tuple-element.5.residual), custom_call_target="tpu_custom_call" | custom-call | tf_op jit(solution)/shard_map/pallas_call | solution.py:302

commit v2 on v1

--- a/solution.py
+++ b/solution.py
@@ -1,4 +1,5 @@
 import functools
+import math
 
 import jax
 import jax.numpy as jnp
@@ -10,6 +11,7 @@
 MESH = pl.DeviceIdType.MESH
 LANES = 128
 CHUNK = 16
+GROUP = 2
 
 
 def round_up(value, step):
@@ -50,16 +52,32 @@
 
     barrier = pltpu.get_barrier_semaphore()
 
-    def place(step):
-        there = 2 * lax.rem(body + step, bodies) + half
+    low_side = row < row_count // 2
+
+    def far(step):
+        return jnp.where(low_side, bodies - 1 - step, step)
+
+    def place(j):
+        there = 2 * j + half
         return {"row": there // col_count, "col": lax.rem(there, col_count)}
 
-    def greet(step, carry):
-        pl.semaphore_signal(barrier, inc=1, device_id=place(step), device_id_type=MESH)
-        return carry
-
+    def each(action):
+        def visit(step, carry):
+            j = far(step)
+
+            @pl.when(j != body)
+            def _():
+                action(j)
+
+            return carry
+
+        lax.fori_loop(0, bodies, visit, 0)
+
+    def greet(j):
+        pl.semaphore_signal(barrier, inc=1, device_id=place(j), device_id_type=MESH)
+
+    each(greet)
     pl.semaphore_signal(barrier, inc=1, device_id={"col": partner}, device_id_type=MESH)
-    lax.fori_loop(1, bodies, greet, 0)
 
     loads = [
         pltpu.make_async_copy(positions_hbm, positions, load_sems.at[0]),
@@ -119,7 +137,7 @@
                 tiles[j, t, a * pad + at : a * pad + at + CHUNK, :] = value.astype(jnp.bfloat16)
         return carry
 
-    first = bodies
+    first = 0
     lax.fori_loop(0, first, build, 0)
     loads[1].wait()
     pl.semaphore_wait(barrier, bodies)
@@ -160,21 +178,17 @@
     forces[body] = force.astype(jnp.bfloat16)
     held[...] = force
 
-    def send(step):
+    def send(j):
         return pltpu.make_async_remote_copy(
             src_ref=forces.at[body],
             dst_ref=forces.at[body],
-            send_sem=send_sems.at[step],
+            send_sem=send_sems.at[j],
             recv_sem=recv_sems.at[body],
-            device_id=place(step),
+            device_id=place(j),
             device_id_type=MESH,
         )
 
-    def start_send(step, carry):
-        send(step).start()
-        return carry
-
-    lax.fori_loop(1, bodies, start_send, 0)
+    each(lambda j: send(j).start())
 
     lax.fori_loop(first, 2 * bodies, build, 0)
 
@@ -186,24 +200,34 @@
             preferred_element_type=jnp.float32,
         )
 
-    def gather(step, total):
-        j = lax.rem(body + step, bodies)
-        pltpu.make_async_remote_copy(
-            src_ref=forces.at[j],
-            dst_ref=forces.at[j],
-            send_sem=send_sems.at[0],
-            recv_sem=recv_sems.at[j],
-            device_id={"col": partner},
-            device_id_type=MESH,
-        ).wait_recv()
-        return total + product(j)
-
-    total = product(body)
+    def receive(j):
+        @pl.when(j != body)
+        def _():
+            pltpu.make_async_remote_copy(
+                src_ref=forces.at[j],
+                dst_ref=forces.at[j],
+                send_sem=send_sems.at[0],
+                recv_sem=recv_sems.at[j],
+                device_id={"col": partner},
+                device_id_type=MESH,
+            ).wait_recv()
+
+    group = math.gcd(bodies, GROUP)
+
+    def gather(turn, total):
+        picks = [far(bodies - 1 - (turn * group + k)) for k in range(group)]
+        for j in picks:
+            receive(j)
+        for j in picks:
+            total = total + product(j)
+        return total
+
+    total = jnp.zeros((slip.shape[0], 6 * pad), jnp.float32)
     if bodies <= 8:
-        for step in range(1, bodies):
-            total = gather(step, total)
+        for turn in range(bodies // group):
+            total = gather(turn, total)
     else:
-        total = lax.fori_loop(1, bodies, gather, total)
+        total = lax.fori_loop(0, bodies // group, gather, total)
     full = round_up(6 * pad, LANES)
     total = jnp.pad(total, ((0, 0), (0, full - 6 * pad)))
     lane = lax.broadcasted_iota(jnp.int32, total.shape, 1)
@@ -223,11 +247,7 @@
     part_swap = swap(part, other_part, part_sems)
     part_swap.start()
 
-    def end_send(step, carry):
-        send(step).wait_send()
-        return carry
-
-    lax.fori_loop(1, bodies, end_send, 0)
+    each(lambda j: send(j).wait_send())
     part_swap.wait()
     mine = slip[...] - (part[half] + other_part[half])[:, :narrow]
     residual[0] = mine

time: 14.1 us -> 13.6 us (0.965)
  Pallas kernels: 13.3 us -> 12.8 us
    pallas_call x1, Pallas kernels: 12.7 us -> 12.1 us  [local(): pl.pallas_call(functools.partial(kernel, row_count, col_count, blobs), ou...]
where the time goes in v2:
time: 13.6 us; the launch traced here: 13.4 us
  Pallas kernels  12.8 us (94%)
  between operations  0.64 us (5%)
    pallas_call x1, Pallas kernels, local(): pl.pallas_call(functools.partial(kernel, row_count, col_count, blobs), ou...  12.1 us
    pallas_call x1, Pallas kernels, local(): pl.pallas_call(finish, out_shape=(jax.ShapeDtypeStruct(slip.shape, f32),)...  0.63 us

profile of v2, /device:TPU:0, one launch (start us, length us, event | category | flops | bytes accessed | tf_op | source)
XLA Modules:
  0.0 13.4 jit_solution(10962895323825435581)
XLA Ops:
  0.6 12.1 %shard_map.50 = (f32[1,16,243]{2,1,0:T(8,128)S(1)}, f32[1,16,243]{2,1,0:T(8,128)S(1)}) custom-call(f32[1,16,243]{2,1,0:T(8,128)} %slip_hbm.1, f32[486,1,243]{2,1,0:T(1,128)} %bitcast.2, f32[3,16,81]{2,1,0:T(8,128)} %bitcast.3), custom_call_target="tpu_custom_call" | custom-call | tf_op jit(solution)/shard_map/pallas_call | solution.py:287
  12.8 0.6 %shard_map.51 = (f32[1,16,243]{2,1,0:T(8,128)}, f32[1,16,243]{2,1,0:T(8,128)}) custom-call(f32[1,16,243]{2,1,0:T(8,128)S(1)} %get-tuple-element.4.updated, f32[1,16,243]{2,1,0:T(8,128)S(1)} %get-tuple-element.5.residual), custom_call_target="tpu_custom_call" | custom-call | tf_op jit(solution)/shard_map/pallas_call | solution.py:322

commit v3 on v2

--- a/solution.py
+++ b/solution.py
@@ -38,7 +38,7 @@
     updated, residual,
     slip, inverse, positions,
     inv_high, inv_low, tiles, own_rows, own, source, other_slip, part, other_part, forces, held,
-    load_sems, slip_sems, part_sems, send_sems, recv_sems,
+    load_sems, slip_sems, part_sems, send_sems, recv_sems, go_sem,
 ):
     bodies = row_count * col_count // 2
     row = lax.axis_index("row")
@@ -73,11 +73,17 @@
 
         lax.fori_loop(0, bodies, visit, 0)
 
-    def greet(j):
-        pl.semaphore_signal(barrier, inc=1, device_id=place(j), device_id_type=MESH)
-
-    each(greet)
-    pl.semaphore_signal(barrier, inc=1, device_id={"col": partner}, device_id_type=MESH)
+    def welcome(j):
+        there = 2 * j
+        device = {"row": there // col_count, "col": lax.rem(there, col_count)}
+        pl.semaphore_signal(barrier, inc=1, device_id=device, device_id_type=MESH)
+
+    each(welcome)
+
+    @pl.when(half == 0)
+    def _():
+        pl.semaphore_signal(barrier, inc=1, device_id={"col": partner}, device_id_type=MESH)
+
 
     loads = [
         pltpu.make_async_copy(positions_hbm, positions, load_sems.at[0]),
@@ -89,29 +95,6 @@
     inv_high[...] = jnp.zeros_like(inv_high)
     inv_low[...] = jnp.zeros_like(inv_low)
     own_rows[...] = jnp.zeros_like(own_rows)
-    loads[0].wait()
-
-    lane = lax.broadcasted_iota(jnp.int32, source.shape[1:], 1)
-    spread = []
-    for a in range(3):
-        rows = jnp.pad(positions[a], ((0, 0), (0, wide - blobs)))
-        spread.append(triple(rows, blobs))
-        source[a] = spread[a]
-        for t in range(2):
-            own_rows[3 * t + a : 3 * t + a + 1, :blobs] = positions[a, pl.ds(2 * body + t, 1), :]
-    source[3] = jnp.where(
-        lane < blobs, spread[0], jnp.where(lane < 2 * blobs, spread[1], spread[2])
-    )
-    own_cols = own_rows[...].T
-    lane = lax.broadcasted_iota(jnp.int32, (pad, wide), 1)
-    for t in range(2):
-        cols = [
-            jnp.broadcast_to(own_cols[:pad, 3 * t + a : 3 * t + a + 1], (pad, wide))
-            for a in range(3)
-        ]
-        for a in range(3):
-            own[t, a] = cols[a]
-        own[t, 3] = jnp.where(lane < blobs, cols[0], jnp.where(lane < 2 * blobs, cols[1], cols[2]))
 
     def build(step, carry):
         j = step // 2
@@ -137,10 +120,7 @@
                 tiles[j, t, a * pad + at : a * pad + at + CHUNK, :] = value.astype(jnp.bfloat16)
         return carry
 
-    first = 0
-    lax.fori_loop(0, first, build, 0)
     loads[1].wait()
-    pl.semaphore_wait(barrier, bodies)
 
     def swap(source_ref, target_ref, sems):
         return pltpu.make_async_remote_copy(
@@ -153,7 +133,16 @@
         )
 
     slip_swap = swap(slip, other_slip, slip_sems)
-    slip_swap.start()
+
+    @pl.when(half == 1)
+    def _():
+        pl.semaphore_wait(barrier, 1)
+        slip_swap.start()
+
+    @pl.when(half == 0)
+    def _():
+        slip_swap.wait_recv()
+        slip_swap.start()
 
     loads[2].wait()
     for h in range(2):
@@ -173,7 +162,12 @@
         return both[:rows] + (both[rows:] + cross)
 
     force = apply(slip[...], half)
-    slip_swap.wait()
+    slip_swap.wait_send()
+
+    @pl.when(half == 1)
+    def _():
+        slip_swap.wait_recv()
+
     force = force + apply(other_slip[...], 1 - half)
     forces[body] = force.astype(jnp.bfloat16)
     held[...] = force
@@ -188,9 +182,42 @@
             device_id_type=MESH,
         )
 
+    @pl.when(half == 0)
+    def _():
+        pl.semaphore_wait(barrier, 2 * (bodies - 1))
+        pl.semaphore_signal(go_sem, inc=1, device_id={"col": partner}, device_id_type=MESH)
+
+    @pl.when(half == 1)
+    def _():
+        pl.semaphore_wait(go_sem, 1)
+
     each(lambda j: send(j).start())
 
-    lax.fori_loop(first, 2 * bodies, build, 0)
+    loads[0].wait()
+
+    lane = lax.broadcasted_iota(jnp.int32, source.shape[1:], 1)
+    spread = []
+    for a in range(3):
+        rows = jnp.pad(positions[a], ((0, 0), (0, wide - blobs)))
+        spread.append(triple(rows, blobs))
+        source[a] = spread[a]
+        for t in range(2):
+            own_rows[3 * t + a : 3 * t + a + 1, :blobs] = positions[a, pl.ds(2 * body + t, 1), :]
+    source[3] = jnp.where(
+        lane < blobs, spread[0], jnp.where(lane < 2 * blobs, spread[1], spread[2])
+    )
+    own_cols = own_rows[...].T
+    lane = lax.broadcasted_iota(jnp.int32, (pad, wide), 1)
+    for t in range(2):
+        cols = [
+            jnp.broadcast_to(own_cols[:pad, 3 * t + a : 3 * t + a + 1], (pad, wide))
+            for a in range(3)
+        ]
+        for a in range(3):
+            own[t, a] = cols[a]
+        own[t, 3] = jnp.where(lane < blobs, cols[0], jnp.where(lane < 2 * blobs, cols[1], cols[2]))
+
+    lax.fori_loop(0, 2 * bodies, build, 0)
 
     def product(j):
         return lax.dot_general(
@@ -312,6 +339,7 @@
             dma((2,)),
             dma((bodies,)),
             dma((bodies,)),
+            pltpu.SemaphoreType.REGULAR,
         ],
         compiler_params=pltpu.CompilerParams(
             collective_id=0,

time: 13.6 us -> 13.4 us (0.985)
  no operation moved by 1% of the time
where the time goes in v3:
time: 13.4 us; the launch traced here: 13.3 us
  Pallas kernels  12.7 us (95%)
  between operations  0.64 us (5%)
    pallas_call x1, Pallas kernels, local(): pl.pallas_call(functools.partial(kernel, row_count, col_count, blobs), ou...  12 us
    pallas_call x1, Pallas kernels, local(): pl.pallas_call(finish, out_shape=(jax.ShapeDtypeStruct(slip.shape, f32),)...  0.63 us

profile of v3, /device:TPU:0, one launch (start us, length us, event | category | flops | bytes accessed | tf_op | source)
XLA Modules:
  0.0 13.3 jit_solution(14428897129993347554)
XLA Ops:
  0.6 12.0 %shard_map.50 = (f32[1,16,243]{2,1,0:T(8,128)S(1)}, f32[1,16,243]{2,1,0:T(8,128)S(1)}) custom-call(f32[1,16,243]{2,1,0:T(8,128)} %slip_hbm.1, f32[486,1,243]{2,1,0:T(1,128)} %bitcast.2, f32[3,16,81]{2,1,0:T(8,128)} %bitcast.3), custom_call_target="tpu_custom_call" | custom-call | tf_op jit(solution)/shard_map/pallas_call | solution.py:314
  12.7 0.6 %shard_map.51 = (f32[1,16,243]{2,1,0:T(8,128)}, f32[1,16,243]{2,1,0:T(8,128)}) custom-call(f32[1,16,243]{2,1,0:T(8,128)S(1)} %get-tuple-element.4.updated, f32[1,16,243]{2,1,0:T(8,128)S(1)} %get-tuple-element.5.residual), custom_call_target="tpu_custom_call" | custom-call | tf_op jit(solution)/shard_map/pallas_call | solution.py:350
